TPU v7x, 32 devices: a whole 2x2x4 slice. The times are simulated.
32 devices in a mesh: wide: 8 (over z, y), narrow: 4 (over x, core).
Axes of the slice: x: 2, y: 2, z: 4, core: 2. Of those that a mesh axis runs over, the one named last changes fastest.
Arguments:
- stem: float32 [2, 8, 4, 512, 128], P(None, 'wide', 'narrow'), may hold values from -6 to 6
- branches: float32 [3, 2, 512, 512], replicated, may hold values from -0.1875 to 0.1875
- mode_order: int32 [3, 9], replicated, may hold values from 0 to 8, each once within a row
Outputs:
- final_stem: float32 [2, 8, 4, 512, 128], P(None, 'wide', 'narrow')
Inputs may be any that keep to these rules, and one draw needn't show every extreme that they name: Each row of mode_order names every mode of 0 to 8 once.
All inputs are finite; a program needn't handle non-finite values.
Results may differ from a plain program's by a relative error of at most 0.0003.
Values may be sent and summed in bfloat16 or wider, within the bound.
No kernel may reach another device: no remote copies, remote signals or barrier semaphores. Data moves between devices by JAX's collectives and lax.ppermute only.
A program may use at most 64 MiB of HBM per device.

v0:
```python
import jax
import jax.numpy as jnp
from jax import lax
from jax.sharding import PartitionSpec as P


def split_pair(values):
    high = values.astype(jnp.bfloat16)
    held = lax.optimization_barrier(high)
    low = (values - held.astype(jnp.float32)).astype(jnp.bfloat16)
    return (high, low)


def expand_order(order, columns):
    column = jnp.arange(columns, dtype=jnp.int32)
    places = jnp.arange(order.shape[0], dtype=jnp.int32)
    bits = jnp.bitwise_and(jnp.right_shift(column[:, None], places[None, :]), 1)
    return jnp.sum(jnp.left_shift(bits, order[None, :]), axis=1)


def prepare(branch_step, order):
    columns = branch_step.shape[1]
    bhigh, blow = split_pair(branch_step)
    inverse_order = jnp.argsort(order)
    inverse = expand_order(inverse_order, columns)
    return (bhigh.reshape(2 * columns, columns), blow.reshape(2 * columns, columns), inverse)


def mult(left, right):
    return lax.dot_general(
        left, right, (((0,), (0,)), ((), ())), preferred_element_type=jnp.float32
    )


def contract(stem_pieces, branch_pieces):
    shigh, slow = stem_pieces
    flat_high, flat_low, inverse = branch_pieces
    shigh = jnp.take(shigh, inverse, axis=1)
    slow = jnp.take(slow, inverse, axis=1)
    rows_count = shigh.shape[2]
    real_high = jnp.concatenate([shigh[0], -shigh[1]], axis=0)
    real_low = jnp.concatenate([slow[0], -slow[1]], axis=0)
    imag_high = jnp.concatenate([shigh[1], shigh[0]], axis=0)
    imag_low = jnp.concatenate([slow[1], slow[0]], axis=0)
    upper = mult(flat_high, jnp.concatenate([real_high, real_low, imag_high, imag_low], axis=1))
    lower = mult(flat_low, jnp.concatenate([real_high, imag_high], axis=1))
    real = upper[:, :rows_count] + upper[:, rows_count : 2 * rows_count] + lower[:, :rows_count]
    imag = (
        upper[:, 2 * rows_count : 3 * rows_count]
        + upper[:, 3 * rows_count :]
        + lower[:, rows_count:]
    )
    return jnp.stack([real, imag])


def body(stem, branches, mode_order):
    columns = stem.shape[3]
    rows_here = stem.shape[4]
    narrow_n = lax.axis_size("narrow")
    wide_n = lax.axis_size("wide")
    local = stem.reshape(2, columns, rows_here)
    first_branch = prepare(branches[0], mode_order[0])
    second_branch = prepare(branches[1], mode_order[1])
    third_branch = prepare(branches[2], mode_order[2])
    first = contract(split_pair(local), first_branch)
    outgoing = first.reshape(2, narrow_n, columns // narrow_n, rows_here)
    received = lax.all_to_all(outgoing, "narrow", split_axis=1, concat_axis=1, tiled=True)
    merged = received.reshape(2, columns, received.shape[3])
    second = contract(split_pair(merged), second_branch)
    outgoing = second.reshape(2, wide_n, columns // wide_n, rows_here)
    received = lax.all_to_all(outgoing, "wide", split_axis=1, concat_axis=1, tiled=True)
    merged = received.reshape(2, columns, received.shape[3])
    final = contract(split_pair(merged), third_branch)
    return final.reshape(2, 1, 1, columns, rows_here)


def solution(mesh):
    return jax.shard_map(
        body,
        mesh=mesh,
        in_specs=(P(None, "wide", "narrow", None, None), P(), P()),
        out_specs=P(None, "wide", "narrow", None, None),
        check_vma=False,
    )
```

profile of v0, /device:TPU:0, one launch (start us, length us, event | category | flops | bytes accessed | tf_op | source)
XLA Modules:
  0.0 81.4 jit_solution(7135167233199474065)
XLA Ops:
  0.0 0.8 slice_bitcast_fusion
  0.8 1.3 %sort.45 = (s32[9]{0:T(128)}, s32[9]{0:T(128)S(1)}) sort(s32[9]{0:T(128)S(1)} %get-tuple-element.52, s32[9]{0:T(128)S(1)} %iota.22), dimensions={0}, to_apply=%region_0.0 | sort | flops 36 | bytes 144 | tf_op jit(solution)/shard_map/jit(argsort)/sort | solution.py:24
  2.2 4.9 %fusion.95 = (bf16[1,2,512,512]{3,2,1,0:T(8,128)(2,1)}, bf16[2,512,512]{2,1,0:T(8,128)(2,1)S(1)}, bf16[2,512,512]{2,1,0:T(8,128)(2,1)S(1)}, bf16[2,512,512]{2,1,...) fusion(f32[3,2,512,512]{3,2,1,0:T(8,128)} %param.6), kind=kLoop, calls=%fused_computation.168 | loop fusion | bytes 9437184 | tf_op jit(solution)/shard_map/slice | solution.py:64
  7.4 1.2 %fusion.74 = bf16[2,512,128]{2,0,1:T(2,128)(2,1)} fusion(bf16[2,512,128]{2,0,1:T(2,128)(2,1)S(1)} %bitcast.121, f32[2,1,1,512,128]{4,3,2,1,0:T(8,128)S(1)} %copy-done), kind=kLoop, calls=%fused_computation.101 | loop fusion | flops 393216 | bytes 1048576 | tf_op jit(solution)/shard_map/convert_element_type | solution.py:10
  8.6 2.4 %gather_fusion = bf16[512,2,128]{2,1,0:T(2,128)(2,1)} fusion(bf16[2,512,128]{2,0,1:T(2,128)(2,1)S(1)} %bitcast.122, s32[1024]{0:T(1024)S(1)} %pad_clamp_fusion.2), kind=kCustom, calls=%fused_computation.clone | custom fusion | bytes 526336 | tf_op jit(solution)/shard_map/jit(_take)/gather | solution.py:38
  11.0 2.3 %gather_fusion.1 = bf16[512,2,128]{2,1,0:T(2,128)(2,1)S(1)} fusion(bf16[2,512,128]{2,0,1:T(2,128)(2,1)} %fusion.74, s32[1024]{0:T(1024)S(1)} %pad_clamp_fusion.2), kind=kCustom, calls=%fused_computation.1.clone | custom fusion | bytes 526336 | tf_op jit(solution)/shard_map/jit(_take)/gather | solution.py:39
  13.3 3.0 %fusion.78 = (bf16[2,512,128]{2,0,1:T(2,128)(2,1)S(1)}, bf16[2,512,128]{2,0,1:T(2,128)(2,1)S(1)}) fusion(bf16[512,2,128]{2,1,0:T(2,128)(2,1)S(1)} %gather_fusion.1, pred[512]{0:T(512)(128)(4,1)S(1)} %compare_and_fusion.2, bf16[512,2,128]{2,1,0:T(2,128)(2,1)} %gather_fusion), kind=kLoop, calls=%fused_computation.123 | loop fusion | flops 262144 | bytes 1049088 | tf_op jit(solution)/shard_map/jit(_take)/select_n | solution.py:39
  17.2 5.3 %fusion.2 = (bf16[2,512,512]{2,1,0:T(8,128)(2,1)S(1)}, bf16[2,512,512]{2,1,0:T(8,128)(2,1)}, bf16[2,512,512]{2,1,0:T(8,128)(2,1)}) fusion(bf16[2,512,512]{2,1,0:T(8,128)(2,1)S(1)} %get-tuple-element.25, f32[3,2,512,512]{3,2,1,0:T(8,128)} %param.6, bf16[2,512,512]{2,1,0:T(8,128)(2,1)S(1)} %get-tuple-element.26, bf16[2,512,512]{2,1,0:T(8,128)(2,1)S(1)} %get-tuple-element.27), kind=kLoop, calls=%fused_computation.14 | loop fusion | flops 4718592 | bytes 12582912 | tf_op jit(solution)/shard_map/convert_element_type | solution.py:10
  23.7 0.8 convolution_bitcast_fusion.2
  24.6 0.8 %pad_maximum_fusion = f32[2,4,128,128]{3,2,0,1:T(8,128)} fusion(f32[1,4,128,128]{3,2,0,1:T(8,128)S(1)} %bitcast.130, f32[1,4,128,128]{3,2,0,1:T(8,128)S(1)} %bitcast.129), kind=kLoop, calls=%fused_computation.74 | loop fusion | flops 131072 | bytes 1048576 | tf_op jit(solution)/shard_map/stack | solution.py:53
  25.4 4.2 %all-to-all-start = ((f32[2,4,128,128]{3,2,0,1:T(8,128)}), f32[2,4,128,128]{3,2,0,1:T(8,128)S(1)}, u32[]{:S(2)}, u32[]{:S(2)}) async-start(f32[2,4,128,128]{3,2,0,1:T(8,128)} %pad_maximum_fusion), calls=%async_computation | async-start | bytes 1048576 | tf_op jit(solution)/shard_map/all_to_all | solution.py:67
  29.6 1.2 %sort.46 = (s32[9]{0:T(128)}, s32[9]{0:T(128)S(1)}) sort(s32[9]{0:T(128)S(1)} %get-tuple-element.53, s32[9]{0:T(128)S(1)} %iota.23), dimensions={0}, to_apply=%region_2.0 | sort | flops 36 | bytes 144 | tf_op jit(solution)/shard_map/jit(argsort)/sort | solution.py:24
  31.0 7.5 %all-to-all-done = f32[2,4,128,128]{3,2,0,1:T(8,128)S(1)} async-done(((f32[2,4,128,128]{3,2,0,1:T(8,128)}), f32[2,4,128,128]{3,2,0,1:T(8,128)S(1)}, u32[]{:S(2)}, u32[]{:S(2)}) %all-to-all-start) | async-done | bytes 524320 | tf_op jit(solution)/shard_map/all_to_all | solution.py:67
  39.4 2.1 %gather_fusion.2 = bf16[512,2,128]{2,1,0:T(2,128)(2,1)S(1)} fusion(bf16[2,512,128]{2,0,1:T(2,128)(2,1)S(1)} %bitcast_convert_fusion.4, s32[1024]{0:T(1024)S(1)} %pad_clamp_fusion.1), kind=kCustom, calls=%fused_computation.2.clone | custom fusion | bytes 526336 | tf_op jit(solution)/shard_map/jit(_take)/gather | solution.py:38
  41.6 2.1 %gather_fusion.3 = bf16[512,2,128]{2,1,0:T(2,128)(2,1)S(1)} fusion(bf16[2,512,128]{2,0,1:T(2,128)(2,1)S(1)} %fusion.73, s32[1024]{0:T(1024)S(1)} %pad_clamp_fusion.1), kind=kCustom, calls=%fused_computation.3.clone | custom fusion | bytes 526336 | tf_op jit(solution)/shard_map/jit(_take)/gather | solution.py:39
  43.7 1.8 %fusion.80 = (bf16[2,512,128]{2,0,1:T(2,128)(2,1)S(1)}, bf16[2,512,128]{2,0,1:T(2,128)(2,1)S(1)}) fusion(bf16[512,2,128]{2,1,0:T(2,128)(2,1)S(1)} %gather_fusion.3, pred[512]{0:T(512)(128)(4,1)S(1)} %compare_and_fusion.1, bf16[512,2,128]{2,1,0:T(2,128)(2,1)S(1)} %gather_fusion.2), kind=kLoop, calls=%fused_computation.125 | loop fusion | flops 262144 | bytes 1049088 | tf_op jit(solution)/shard_map/jit(_take)/select_n | solution.py:39
  48.5 0.8 %pad_maximum_fusion.1 = f32[2,8,64,128]{3,2,0,1:T(8,128)} fusion(f32[1,8,64,128]{3,2,0,1:T(8,128)S(1)} %bitcast.132, f32[1,8,64,128]{3,2,0,1:T(8,128)S(1)} %bitcast.131), kind=kLoop, calls=%fused_computation.83 | loop fusion | flops 131072 | bytes 1048576 | tf_op jit(solution)/shard_map/stack | solution.py:53
  49.3 6.5 %all-to-all-start.1 = ((f32[2,8,64,128]{3,2,0,1:T(8,128)}), f32[2,8,64,128]{3,2,0,1:T(8,128)S(1)}, u32[]{:S(2)}, u32[]{:S(2)}) async-start(f32[2,8,64,128]{3,2,0,1:T(8,128)} %pad_maximum_fusion.1), calls=%async_computation.1 | async-start | bytes 1048576 | tf_op jit(solution)/shard_map/all_to_all | solution.py:71
  55.8 1.3 %sort.47 = (s32[9]{0:T(128)}, s32[9]{0:T(128)S(1)}) sort(s32[9]{0:T(128)S(1)} %get-tuple-element.51, s32[9]{0:T(128)S(1)} %iota.24), dimensions={0}, to_apply=%region_4.6 | sort | flops 36 | bytes 144 | tf_op jit(solution)/shard_map/jit(argsort)/sort | solution.py:24
  57.2 12.8 %all-to-all-done.1 = f32[2,8,64,128]{3,2,0,1:T(8,128)S(1)} async-done(((f32[2,8,64,128]{3,2,0,1:T(8,128)}), f32[2,8,64,128]{3,2,0,1:T(8,128)S(1)}, u32[]{:S(2)}, u32[]{:S(2)}) %all-to-all-start.1) | async-done | bytes 524320 | tf_op jit(solution)/shard_map/all_to_all | solution.py:71
  71.0 2.1 %gather_fusion.4 = bf16[512,2,128]{2,1,0:T(2,128)(2,1)S(1)} fusion(bf16[2,512,128]{2,0,1:T(2,128)(2,1)S(1)} %bitcast_convert_fusion.3, s32[1024]{0:T(1024)S(1)} %pad_clamp_fusion), kind=kCustom, calls=%fused_computation.4.clone | custom fusion | bytes 526336 | tf_op jit(solution)/shard_map/jit(_take)/gather | solution.py:38
  73.1 2.1 %gather_fusion.5 = bf16[512,2,128]{2,1,0:T(2,128)(2,1)S(1)} fusion(bf16[2,512,128]{2,0,1:T(2,128)(2,1)S(1)} %fusion.72, s32[1024]{0:T(1024)S(1)} %pad_clamp_fusion), kind=kCustom, calls=%fused_computation.5.clone | custom fusion | bytes 526336 | tf_op jit(solution)/shard_map/jit(_take)/gather | solution.py:39
  75.2 1.8 %fusion.82 = (bf16[2,512,128]{2,0,1:T(2,128)(2,1)S(1)}, bf16[2,512,128]{2,0,1:T(2,128)(2,1)S(1)}) fusion(bf16[512,2,128]{2,1,0:T(2,128)(2,1)S(1)} %gather_fusion.5, pred[512]{0:T(512)(128)(4,1)S(1)} %compare_and_fusion, bf16[512,2,128]{2,1,0:T(2,128)(2,1)S(1)} %gather_fusion.4), kind=kLoop, calls=%fused_computation.127 | loop fusion | flops 262144 | bytes 1049088 | tf_op jit(solution)/shard_map/jit(_take)/select_n | solution.py:39
  80.4 1.0 %copy.68 = f32[2,1,1,512,128]{4,3,2,1,0:T(8,128)} copy(f32[2,1,1,512,128]{3,4,0,2,1:T(8,128)S(1)} %maximum_bitcast_fusion) | data formatting | bytes 1048576 | tf_op jit(solution)/shard_map/reshape | solution.py:74
  (60 shorter events, 11.0 us)
Async XLA Ops:
  2.2 4.9 %copy-start = (f32[2,1,1,512,128]{4,3,2,1,0:T(8,128)S(1)}, f32[2,1,1,512,128]{4,3,2,1,0:T(8,128)}, u32[]{:S(2)}) copy-start(f32[2,1,1,512,128]{4,3,2,1,0:T(8,128)} %param.5) | copy-start | bytes 1572868
  22.5 1.2 %copy-start.5 = (bf16[1,2,512,512]{3,2,1,0:T(8,128)(2,1)S(1)}, bf16[1,2,512,512]{3,2,1,0:T(8,128)(2,1)}, u32[]{:S(2)}) copy-start(bf16[1,2,512,512]{3,2,1,0:T(8,128)(2,1)} %get-tuple-element.28) | copy-start | bytes 3145732
  25.4 13.1 %all-to-all-start = ((f32[2,4,128,128]{3,2,0,1:T(8,128)}), f32[2,4,128,128]{3,2,0,1:T(8,128)S(1)}, u32[]{:S(2)}, u32[]{:S(2)}) async-start(f32[2,4,128,128]{3,2,0,1:T(8,128)} %pad_maximum_fusion), calls=%async_computation | async-start | bytes 1048576 | tf_op jit(solution)/shard_map/all_to_all | solution.py:67
  45.5 1.2 %copy-start.4 = (bf16[2,512,512]{2,1,0:T(8,128)(2,1)S(1)}, bf16[2,512,512]{2,1,0:T(8,128)(2,1)}, u32[]{:S(2)}) copy-start(bf16[2,512,512]{2,1,0:T(8,128)(2,1)} %get-tuple-element.31) | copy-start | bytes 3145732
  46.3 1.3 %copy-start.3 = (bf16[1,2,512,512]{3,2,1,0:T(8,128)(2,1)S(1)}, bf16[1,2,512,512]{3,2,1,0:T(8,128)(2,1)}, u32[]{:S(2)}) copy-start(bf16[1,2,512,512]{3,2,1,0:T(8,128)(2,1)} %get-tuple-element.29) | copy-start | bytes 3145732
  49.3 20.7 %all-to-all-start.1 = ((f32[2,8,64,128]{3,2,0,1:T(8,128)}), f32[2,8,64,128]{3,2,0,1:T(8,128)S(1)}, u32[]{:S(2)}, u32[]{:S(2)}) async-start(f32[2,8,64,128]{3,2,0,1:T(8,128)} %pad_maximum_fusion.1), calls=%async_computation.1 | async-start | bytes 1048576 | tf_op jit(solution)/shard_map/all_to_all | solution.py:71
  77.0 1.2 %copy-start.2 = (bf16[2,512,512]{2,1,0:T(8,128)(2,1)S(1)}, bf16[2,512,512]{2,1,0:T(8,128)(2,1)}, u32[]{:S(2)}) copy-start(bf16[2,512,512]{2,1,0:T(8,128)(2,1)} %get-tuple-element.32) | copy-start | bytes 3145732
  78.2 1.2 %copy-start.1 = (bf16[1,2,512,512]{3,2,1,0:T(8,128)(2,1)S(1)}, bf16[1,2,512,512]{3,2,1,0:T(8,128)(2,1)}, u32[]{:S(2)}) copy-start(bf16[1,2,512,512]{3,2,1,0:T(8,128)(2,1)} %get-tuple-element.24) | copy-start | bytes 3145732
where the time goes:
time: 81.9 us; the launch traced here: 81.4 us
  local copies, waits for them, and re-layouts  25.9 us (32%)
  other arithmetic  20.5 us (25%)
  waiting for transfers between devices  20.3 us (25%)
  starting transfers between devices  10.7 us (13%)
  matrix products  3.67 us (4%)
    all_to_all x1, waiting for transfers between devices, body(): lax.all_to_all(outgoing, 'wide', split_axis=1, concat_axis=1, tiled=True)  12.8 us
    all_to_all x1, waiting for transfers between devices, body(): lax.all_to_all(outgoing, 'narrow', split_axis=1, concat_axis=1, tiled=True)  7.53 us
    convert_element_type x4, other arithmetic, split_pair(): low = (values - held.astype(jnp.float32)).astype(jnp.bfloat16)  7.11 us
    gather x3, local copies, waits for them, and re-layouts, contract(): shigh = jnp.take(shigh, inverse, axis=1)  6.6 us
    select_n x3, other arithmetic, contract(): slow = jnp.take(slow, inverse, axis=1)  6.55 us
    gather x3, local copies, waits for them, and re-layouts, contract(): slow = jnp.take(slow, inverse, axis=1)  6.53 us
    all_to_all x1, starting transfers between devices, body(): lax.all_to_all(outgoing, 'wide', split_axis=1, concat_axis=1, tiled=True)  6.47 us
    slice x1, local copies, waits for them, and re-layouts, body(): third_branch = prepare(branches[2], mode_order[2])  4.86 us
  transfers between devices with their start and end apart: 2, of which 2 were waited for; matrix products, arithmetic and copies ran while one was open for 3% of the time, Pallas kernels for 0%

commit v1 on v0

--- a/solution.py
+++ b/solution.py
@@ -68,7 +68,10 @@
     merged = received.reshape(2, columns, received.shape[3])
     second = contract(split_pair(merged), second_branch)
     outgoing = second.reshape(2, wide_n, columns // wide_n, rows_here)
-    received = lax.all_to_all(outgoing, "wide", split_axis=1, concat_axis=1, tiled=True)
+    received = jnp.concatenate(
+        lax.all_to_all(jnp.stack(jnp.split(outgoing, lax.axis_size("wide"), axis=1)), "wide", 0, 0),
+        axis=1,
+    )
     merged = received.reshape(2, columns, received.shape[3])
     final = contract(split_pair(merged), third_branch)
     return final.reshape(2, 1, 1, columns, rows_here)

time: 81.9 us -> 87.3 us (1.066)
  other arithmetic: 20.5 us -> 24.2 us
  waiting for transfers between devices: 20.3 us -> 21.7 us
    unnamed x0 -> x7, other arithmetic: none -> 4.44 us
    all_to_all x1, waiting for transfers between devices: 12.8 us -> 14.2 us  [body(): lax.all_to_all(jnp.stack(jnp.split(outgoing, lax.axis_size('wide'), axis=...]
    another operation x3 -> x2, other arithmetic: 1.82 us -> 0.98 us  [contract(): return jnp.stack([real, imag])]
  transfers between devices with their start and end apart: 2 -> 2, of which waited for: 2 -> 2; matrix products, arithmetic and copies ran while one was open for 3% -> 2% of each run, Pallas kernels for 0% -> 0%
where the time goes in v1:
time: 87.3 us; the launch traced here: 86.7 us
  local copies, waits for them, and re-layouts  26.1 us (30%)
  other arithmetic  24.2 us (28%)
  waiting for transfers between devices  21.7 us (25%)
  starting transfers between devices  10.7 us (12%)
  matrix products  3.66 us (4%)
    all_to_all x1, waiting for transfers between devices, body(): lax.all_to_all(jnp.stack(jnp.split(outgoing, lax.axis_size('wide'), axis=...  14.2 us
    all_to_all x1, waiting for transfers between devices, body(): lax.all_to_all(outgoing, 'narrow', split_axis=1, concat_axis=1, tiled=True)  7.49 us
    convert_element_type x4, other arithmetic, split_pair(): low = (values - held.astype(jnp.float32)).astype(jnp.bfloat16)  6.87 us
    gather x3, local copies, waits for them, and re-layouts, contract(): shigh = jnp.take(shigh, inverse, axis=1)  6.6 us
    select_n x3, other arithmetic, contract(): slow = jnp.take(slow, inverse, axis=1)  6.54 us
    gather x3, local copies, waits for them, and re-layouts, contract(): slow = jnp.take(slow, inverse, axis=1)  6.53 us
    all_to_all x1, starting transfers between devices, body(): lax.all_to_all(jnp.stack(jnp.split(outgoing, lax.axis_size('wide'), axis=...  6.47 us
    slice x1, local copies, waits for them, and re-layouts, body(): third_branch = prepare(branches[2], mode_order[2])  4.86 us
  transfers between devices with their start and end apart: 2, of which 2 were waited for; matrix products, arithmetic and copies ran while one was open for 2% of the time, Pallas kernels for 0%

profile of v1, /device:TPU:0, one launch (start us, length us, event | category | flops | bytes accessed | tf_op | source)
XLA Modules:
  0.0 86.7 jit_solution(8210169564710069178)
XLA Ops:
  0.0 0.8 slice_bitcast_fusion
  0.8 1.3 %sort.45 = (s32[9]{0:T(128)}, s32[9]{0:T(128)S(1)}) sort(s32[9]{0:T(128)S(1)} %get-tuple-element.52, s32[9]{0:T(128)S(1)} %iota.22), dimensions={0}, to_apply=%region_0.0 | sort | flops 36 | bytes 144 | tf_op jit(solution)/shard_map/jit(argsort)/sort | solution.py:24
  2.2 4.9 %fusion.117 = (bf16[1,2,512,512]{3,2,1,0:T(8,128)(2,1)}, bf16[2,512,512]{2,1,0:T(8,128)(2,1)S(1)}, bf16[2,512,512]{2,1,0:T(8,128)(2,1)S(1)}, bf16[2,512,512]{2,1...) fusion(f32[3,2,512,512]{3,2,1,0:T(8,128)} %param.6), kind=kLoop, calls=%fused_computation.203 | loop fusion | bytes 9437184 | tf_op jit(solution)/shard_map/slice | solution.py:64
  7.4 1.2 %fusion.73 = bf16[2,512,128]{2,0,1:T(2,128)(2,1)} fusion(bf16[2,512,128]{2,0,1:T(2,128)(2,1)S(1)} %bitcast.169, f32[2,1,1,512,128]{4,3,2,1,0:T(8,128)S(1)} %copy-done), kind=kLoop, calls=%fused_computation.111 | loop fusion | flops 393216 | bytes 1048576 | tf_op jit(solution)/shard_map/convert_element_type | solution.py:10
  8.6 1.2 %sort.47 = (s32[9]{0:T(128)}, s32[9]{0:T(128)S(1)}) sort(s32[9]{0:T(128)S(1)} %get-tuple-element.51, s32[9]{0:T(128)S(1)} %iota.24), dimensions={0}, to_apply=%region_4.6 | sort | flops 36 | bytes 144 | tf_op jit(solution)/shard_map/jit(argsort)/sort | solution.py:24
  10.0 2.4 %gather_fusion = bf16[512,2,128]{2,1,0:T(2,128)(2,1)} fusion(bf16[2,512,128]{2,0,1:T(2,128)(2,1)S(1)} %bitcast.170, s32[1024]{0:T(1024)S(1)} %get-tuple-element.61), kind=kCustom, calls=%fused_computation.clone | custom fusion | bytes 526336 | tf_op jit(solution)/shard_map/jit(_take)/gather | solution.py:38
  12.3 2.3 %gather_fusion.1 = bf16[512,2,128]{2,1,0:T(2,128)(2,1)S(1)} fusion(bf16[2,512,128]{2,0,1:T(2,128)(2,1)} %fusion.73, s32[1024]{0:T(1024)S(1)} %get-tuple-element.61), kind=kCustom, calls=%fused_computation.1.clone | custom fusion | bytes 526336 | tf_op jit(solution)/shard_map/jit(_take)/gather | solution.py:39
  14.6 3.0 %fusion.77 = (bf16[2,512,128]{2,0,1:T(2,128)(2,1)S(1)}, bf16[2,512,128]{2,0,1:T(2,128)(2,1)S(1)}) fusion(bf16[512,2,128]{2,1,0:T(2,128)(2,1)S(1)} %gather_fusion.1, pred[512]{0:T(512)(128)(4,1)S(1)} %compare_and_fusion.2, bf16[512,2,128]{2,1,0:T(2,128)(2,1)} %gather_fusion), kind=kLoop, calls=%fused_computation.134 | loop fusion | flops 262144 | bytes 1049088 | tf_op jit(solution)/shard_map/jit(_take)/select_n | solution.py:39
  18.5 5.3 %fusion.2 = (bf16[2,512,512]{2,1,0:T(8,128)(2,1)S(1)}, bf16[2,512,512]{2,1,0:T(8,128)(2,1)}, bf16[2,512,512]{2,1,0:T(8,128)(2,1)}) fusion(bf16[2,512,512]{2,1,0:T(8,128)(2,1)S(1)} %get-tuple-element.25, f32[3,2,512,512]{3,2,1,0:T(8,128)} %param.6, bf16[2,512,512]{2,1,0:T(8,128)(2,1)S(1)} %get-tuple-element.26, bf16[2,512,512]{2,1,0:T(8,128)(2,1)S(1)} %get-tuple-element.27), kind=kLoop, calls=%fused_computation.14 | loop fusion | flops 4718592 | bytes 12582912 | tf_op jit(solution)/shard_map/convert_element_type | solution.py:10
  25.1 0.8 convolution_bitcast_fusion.2
  25.9 0.8 pad_maximum_fusion
  26.7 4.2 %all-to-all-start = ((f32[2,4,128,128]{3,2,0,1:T(8,128)}), f32[2,4,128,128]{3,2,0,1:T(8,128)S(1)}, u32[]{:S(2)}, u32[]{:S(2)}) async-start(f32[2,4,128,128]{3,2,0,1:T(8,128)} %pad_maximum_fusion), calls=%async_computation | async-start | bytes 1048576 | tf_op jit(solution)/shard_map/all_to_all | solution.py:67
  31.0 1.3 %sort.46 = (s32[9]{0:T(128)}, s32[9]{0:T(128)S(1)}) sort(s32[9]{0:T(128)S(1)} %get-tuple-element.53, s32[9]{0:T(128)S(1)} %iota.23), dimensions={0}, to_apply=%region_2.0 | sort | flops 36 | bytes 144 | tf_op jit(solution)/shard_map/jit(argsort)/sort | solution.py:24
  32.3 7.5 %all-to-all-done = f32[2,4,128,128]{3,2,0,1:T(8,128)S(1)} async-done(((f32[2,4,128,128]{3,2,0,1:T(8,128)}), f32[2,4,128,128]{3,2,0,1:T(8,128)S(1)}, u32[]{:S(2)}, u32[]{:S(2)}) %all-to-all-start) | async-done | bytes 524320 | tf_op jit(solution)/shard_map/all_to_all | solution.py:67
  40.8 2.1 %gather_fusion.2 = bf16[512,2,128]{2,1,0:T(2,128)(2,1)S(1)} fusion(bf16[2,512,128]{2,0,1:T(2,128)(2,1)S(1)} %bitcast_convert_fusion.3, s32[1024]{0:T(1024)S(1)} %pad_clamp_fusion.1), kind=kCustom, calls=%fused_computation.2.clone | custom fusion | bytes 526336 | tf_op jit(solution)/shard_map/jit(_take)/gather | solution.py:38
  42.9 2.1 %gather_fusion.3 = bf16[512,2,128]{2,1,0:T(2,128)(2,1)S(1)} fusion(bf16[2,512,128]{2,0,1:T(2,128)(2,1)S(1)} %fusion.72, s32[1024]{0:T(1024)S(1)} %pad_clamp_fusion.1), kind=kCustom, calls=%fused_computation.3.clone | custom fusion | bytes 526336 | tf_op jit(solution)/shard_map/jit(_take)/gather | solution.py:39
  45.0 1.8 %fusion.79 = (bf16[2,512,128]{2,0,1:T(2,128)(2,1)S(1)}, bf16[2,512,128]{2,0,1:T(2,128)(2,1)S(1)}) fusion(bf16[512,2,128]{2,1,0:T(2,128)(2,1)S(1)} %gather_fusion.3, pred[512]{0:T(512)(128)(4,1)S(1)} %compare_and_fusion.1, bf16[512,2,128]{2,1,0:T(2,128)(2,1)S(1)} %gather_fusion.2), kind=kLoop, calls=%fused_computation.136 | loop fusion | flops 262144 | bytes 1049088 | tf_op jit(solution)/shard_map/jit(_take)/select_n | solution.py:39
  49.0 0.7 convolution_bitcast_fusion.1
  54.9 6.5 %all-to-all-start.1 = ((f32[8,2,1,64,128]{4,3,1,2,0:T(8,128)}), f32[8,2,1,64,128]{4,3,1,2,0:T(8,128)S(1)}, u32[]{:S(2)}, u32[]{:S(2)}) async-start(f32[8,2,1,64,128]{4,3,1,2,0:T(8,128)} %fusion.104), calls=%async_computation.1 | async-start | bytes 1048576 | tf_op jit(solution)/shard_map/all_to_all | solution.py:72
  61.4 14.2 %all-to-all-done.1 = f32[8,2,1,64,128]{4,3,1,2,0:T(8,128)S(1)} async-done(((f32[8,2,1,64,128]{4,3,1,2,0:T(8,128)}), f32[8,2,1,64,128]{4,3,1,2,0:T(8,128)S(1)}, u32[]{:S(2)}, u32[]{:S(2)}) %all-to-all-start.1) | async-done | bytes 524320 | tf_op jit(solution)/shard_map/all_to_all | solution.py:72
  76.3 2.1 %gather_fusion.5 = bf16[512,2,128]{2,1,0:T(2,128)(2,1)S(1)} fusion(bf16[2,512,128]{2,0,1:T(2,128)(2,1)S(1)} %copy.137, s32[1024]{0:T(1024)S(1)} %get-tuple-element.60), kind=kCustom, calls=%fused_computation.5.clone | custom fusion | bytes 526336 | tf_op jit(solution)/shard_map/jit(_take)/gather | solution.py:39
  78.4 2.1 %gather_fusion.4 = bf16[512,2,128]{2,1,0:T(2,128)(2,1)S(1)} fusion(bf16[2,512,128]{2,0,1:T(2,128)(2,1)S(1)} %copy.136, s32[1024]{0:T(1024)S(1)} %get-tuple-element.60), kind=kCustom, calls=%fused_computation.4.clone | custom fusion | bytes 526336 | tf_op jit(solution)/shard_map/jit(_take)/gather | solution.py:38
  80.6 1.8 %fusion.81 = (bf16[2,512,128]{2,0,1:T(2,128)(2,1)S(1)}, bf16[2,512,128]{2,0,1:T(2,128)(2,1)S(1)}) fusion(bf16[512,2,128]{2,1,0:T(2,128)(2,1)S(1)} %gather_fusion.5, pred[512]{0:T(512)(128)(4,1)S(1)} %compare_and_fusion, bf16[512,2,128]{2,1,0:T(2,128)(2,1)S(1)} %gather_fusion.4), kind=kLoop, calls=%fused_computation.138 | loop fusion | flops 262144 | bytes 1049088 | tf_op jit(solution)/shard_map/jit(_take)/select_n | solution.py:39
  85.7 1.0 %copy.140 = f32[2,1,1,512,128]{4,3,2,1,0:T(8,128)} copy(f32[2,1,1,512,128]{3,4,0,2,1:T(8,128)S(1)} %maximum_bitcast_fusion) | data formatting | bytes 1048576 | tf_op jit(solution)/shard_map/reshape | solution.py:77
  (69 shorter events, 15.0 us)
Async XLA Ops:
  2.2 4.9 %copy-start = (f32[2,1,1,512,128]{4,3,2,1,0:T(8,128)S(1)}, f32[2,1,1,512,128]{4,3,2,1,0:T(8,128)}, u32[]{:S(2)}) copy-start(f32[2,1,1,512,128]{4,3,2,1,0:T(8,128)} %param.5) | copy-start | bytes 1572868
  23.8 1.2 %copy-start.5 = (bf16[1,2,512,512]{3,2,1,0:T(8,128)(2,1)S(1)}, bf16[1,2,512,512]{3,2,1,0:T(8,128)(2,1)}, u32[]{:S(2)}) copy-start(bf16[1,2,512,512]{3,2,1,0:T(8,128)(2,1)} %get-tuple-element.28) | copy-start | bytes 3145732
  26.7 13.1 %all-to-all-start = ((f32[2,4,128,128]{3,2,0,1:T(8,128)}), f32[2,4,128,128]{3,2,0,1:T(8,128)S(1)}, u32[]{:S(2)}, u32[]{:S(2)}) async-start(f32[2,4,128,128]{3,2,0,1:T(8,128)} %pad_maximum_fusion), calls=%async_computation | async-start | bytes 1048576 | tf_op jit(solution)/shard_map/all_to_all | solution.py:67
  46.8 1.2 %copy-start.4 = (bf16[2,512,512]{2,1,0:T(8,128)(2,1)S(1)}, bf16[2,512,512]{2,1,0:T(8,128)(2,1)}, u32[]{:S(2)}) copy-start(bf16[2,512,512]{2,1,0:T(8,128)(2,1)} %get-tuple-element.31) | copy-start | bytes 3145732
  47.7 1.3 %copy-start.3 = (bf16[1,2,512,512]{3,2,1,0:T(8,128)(2,1)S(1)}, bf16[1,2,512,512]{3,2,1,0:T(8,128)(2,1)}, u32[]{:S(2)}) copy-start(bf16[1,2,512,512]{3,2,1,0:T(8,128)(2,1)} %get-tuple-element.29) | copy-start | bytes 3145732
  54.9 20.7 %all-to-all-start.1 = ((f32[8,2,1,64,128]{4,3,1,2,0:T(8,128)}), f32[8,2,1,64,128]{4,3,1,2,0:T(8,128)S(1)}, u32[]{:S(2)}, u32[]{:S(2)}) async-start(f32[8,2,1,64,128]{4,3,1,2,0:T(8,128)} %fusion.104), calls=%async_computation.1 | async-start | bytes 1048576 | tf_op jit(solution)/shard_map/all_to_all | solution.py:72
  82.4 1.2 %copy-start.2 = (bf16[2,512,512]{2,1,0:T(8,128)(2,1)S(1)}, bf16[2,512,512]{2,1,0:T(8,128)(2,1)}, u32[]{:S(2)}) copy-start(bf16[2,512,512]{2,1,0:T(8,128)(2,1)} %get-tuple-element.32) | copy-start | bytes 3145732
  83.6 1.2 %copy-start.1 = (bf16[1,2,512,512]{3,2,1,0:T(8,128)(2,1)S(1)}, bf16[1,2,512,512]{3,2,1,0:T(8,128)(2,1)}, u32[]{:S(2)}) copy-start(bf16[1,2,512,512]{3,2,1,0:T(8,128)(2,1)} %get-tuple-element.24) | copy-start | bytes 3145732
